TPU v7x, 512 devices: a whole 4x4x16 slice. The times are simulated.
512 devices in a mesh: voxel: 32 (over x, z_lo, core), feature: 4 (over z_hi), tm: 4 (over y).
Axes of the slice: x: 4, y: 4, z: 16 (z_hi: 4, z_lo: 4; z = z_hi * 4 + z_lo), core: 2. Of those that a mesh axis runs over, the one named last changes fastest.
Arguments:
- hidden: bfloat16 [3072, 8192], P('tm', 'feature'), may hold values from -6 to 6
- bold: bfloat16 [3072, 4096], P('tm', 'voxel'), may hold values from -6 to 6
- panel: bfloat16 [65536, 128], P(('feature', 'tm'), 'voxel'), may hold values from -0.0234375 to 0.0234375
- eigvals: float32 [128], replicated, may hold values from 0.05 to 2
- ridge_grid: int32 [24], replicated, may hold values from 0 to 16
- delays: int32 [8], replicated, may hold values from 1 to 12, as said below
- runs: int32 [3072], replicated, may hold values from 0 to 7, never falling along the last dimension, each value on 1 to 768 neighbouring positions
Outputs:
- scaled: bfloat16 [24, 128, 4096], P(None, None, 'voxel')
Inputs may be any that keep to these rules, and one draw needn't show every extreme that they name: 8 distinct delays, 12 among them. `runs`: run numbers never fall along the TRs; a run holds 1 to 768 TRs.
All inputs are finite; a program needn't handle non-finite values.
Results may differ from a plain program's by a relative error of at most 0.022.
Values may be sent and summed in bfloat16 or wider, within the bound.
A program may use at most 64 MiB of HBM per device.

v0:
```python
import math
import jax
import jax.numpy as jnp
from jax import lax
from jax.sharding import PartitionSpec as P

DELAYS = 8
MAXD = 12


def passed_along(value, axis, steps):
    count = lax.axis_size(axis)
    first, last = (max(0, -steps), min(count, count - steps))
    return lax.ppermute(value, axis, [(source, source + steps) for source in range(first, last)])


def contract_rows(left, right):
    return lax.dot_general(
        left, right, (((0,), (0,)), ((), ())), preferred_element_type=jnp.float32
    )


def shards(hidden, bold, panel, eigvals, ridge_grid, delays, runs):
    t_rows = hidden.shape[0]
    d_local = hidden.shape[1]
    v_cols = bold.shape[1]
    total_rows = t_rows * lax.axis_size("tm")
    first = lax.axis_index("tm") * t_rows
    ahead = passed_along(bold[:MAXD], "tm", -1)
    extended = jnp.concatenate([bold, ahead], 0)
    runs_pad = jnp.concatenate([runs, jnp.full((MAXD,), -1, jnp.int32)])
    own_runs = lax.dynamic_slice_in_dim(runs, first, t_rows)
    positions = first + jnp.arange(t_rows, dtype=jnp.int32)
    lagged_list = []
    for slot in range(DELAYS):
        offset = delays[slot]
        target_runs = lax.dynamic_slice_in_dim(runs_pad, first + offset, t_rows)
        valid = (positions + offset < total_rows) & (target_runs == own_runs)
        moved = lax.dynamic_slice_in_dim(extended, offset, t_rows, 0)
        lagged_list.append(jnp.where(valid[:, None], moved, jnp.zeros_like(moved)))
    stacked = jnp.stack(lagged_list, 1).reshape(t_rows, DELAYS * v_cols)
    cross = contract_rows(hidden, stacked)
    partial_cov = cross.reshape(d_local * DELAYS, v_cols).astype(jnp.bfloat16)
    panel_rows = lax.all_gather(panel, "tm", axis=0, tiled=True)
    rotated_part = contract_rows(
        lax.all_gather(panel_rows, "voxel", axis=1, tiled=True), partial_cov
    )
    rotated = lax.psum(rotated_part.astype(jnp.bfloat16), ("feature", "tm")).astype(jnp.float32)
    penalty = 2.0 ** ((ridge_grid.astype(jnp.float32) - 8.0) * 0.5)
    scaled = rotated[None] / (
        math.sqrt(total_rows) * (eigvals[None, :, None] + penalty[:, None, None])
    )
    return scaled.astype(jnp.bfloat16)


def solution(mesh):
    return jax.shard_map(
        shards,
        mesh=mesh,
        in_specs=(
            P("tm", "feature"),
            P("tm", "voxel"),
            P(("feature", "tm"), "voxel"),
            P(),
            P(),
            P(),
            P(),
        ),
        out_specs=P(None, None, "voxel"),
        check_vma=False,
    )
```

profile of v0, /device:TPU:2, one launch (start us, length us, event | category | flops | bytes accessed | tf_op | source)
XLA Modules:
  0.0 209.7 jit_solution(480760499588680285)
XLA Ops:
  6.5 14.4 %all_gather.6 = bf16[16384,4]{0,1:T(4,128)(2,1)} all-gather(bf16[4096,4]{0,1:T(4,128)(2,1)} %param.9), channel_id=1, replica_groups=mesh['voxel'=32,'feature'=4,'tm'=4] {'tm'}, dimensions={0}, use_global_device_ids=true | all-gather | bytes 163840 | tf_op jit(solution)/shard_map/all_gather | solution.py:44
  20.9 0.7 slice.28
  21.8 1.3 collective-permute-start
  23.1 1.6 fusion.49
  29.6 4.1 %fusion.48 = (pred[768]{0:T(1024)(128)(4,1)S(1)}, pred[768]{0:T(1024)(128)(4,1)S(1)}, pred[768]{0:T(1024)(128)(4,1)S(1)}, pred[768]{0:T(1024)(128)(4,1)S(1)}, pred[768]{0:T(1024)(128)(4,1)S(1)}) fusion(s32[]{:T(128)S(6)} %select_n.98, s32[3072]{0:T(1024)} %param.13, s32[]{:T(128)} %bitcast.14, s32[]{:T(128)S(6)} %mul.17, s32[]{:T(128)S(6)} %select_n.77, ...), kind=kLoop, calls=%fused_computation.77 | loop fusion | flops 16128 | bytes 22812 | tf_op jit(solution)/shard_map/and | solution.py:38
  33.7 0.7 multiply_power_fusion
  34.4 0.7 add_multiply_fusion
  35.1 2.7 %fusion.47 = (pred[768]{0:T(1024)(128)(4,1)S(1)}, pred[768]{0:T(1024)(128)(4,1)S(1)}, pred[768]{0:T(1024)(128)(4,1)S(1)}) fusion(s32[]{:T(128)S(6)} %select_n.95, s32[3072]{0:T(1024)} %param.13, s32[]{:T(128)} %bitcast.12, s32[]{:T(128)S(6)} %mul.17, s32[]{:T(128)S(6)} %select_n.77, s32[]{:T(128)S(6)} %select_n.80, s32[]{:T(128)} %bitcast.2, ...), kind=kLoop, calls=%fused_computation.76 | loop fusion | flops 9984 | bytes 20244 | tf_op jit(solution)/shard_map/and | solution.py:38
  38.5 1.1 copy.14
  53.9 0.2 fusion.12
  54.1 0.2 fusion.16
  54.3 0.2 fusion.20
  54.5 0.2 fusion.24
  54.7 0.2 fusion.28
  54.9 0.2 fusion.32
  55.1 0.2 fusion.4
  55.3 5.0 %convert_bitcast_fusion = bf16[2048,1024]{0,1:T(8,128)(2,1)} fusion(bf16[768,1024]{0,1:T(8,128)(2,1)S(1)} %bitcast.53, bf16[768,2048]{1,0:T(8,128)(2,1)S(1)} %copy-done), kind=kOutput, calls=%fused_computation | convolution fusion | flops 3223322624 | bytes 8912896 | tf_op jit(solution)/shard_map/dot_general | solution.py:18
  60.3 6.4 %copy.15 = bf16[2048,1024]{1,0:T(8,128)(2,1)} copy(bf16[2048,1024]{0,1:T(8,128)(2,1)} %convert_bitcast_fusion) | data formatting | bytes 8388608 | tf_op jit(solution)/shard_map/convert_element_type | solution.py:43
  66.7 7.4 %convert_element_type.26 = bf16[16384,128]{1,0:T(8,128)(2,1)} reshape(bf16[2048,1024]{1,0:T(8,128)(2,1)} %copy.15) | data formatting | bytes 8388608 | tf_op jit(solution)/shard_map/convert_element_type | solution.py:43
  74.1 17.7 %all-gather.3.cloned.1.call-done = bf16[32,4,16384]{2,1,0:T(4,128)(2,1)} async-done(((bf16[1,4,16384]{2,1,0:T(4,128)(2,1)}), bf16[32,4,16384]{2,1,0:T(4,128)(2,1)}) %all-gather.3.cloned.1.call-update) | async-done | bytes 4194320 | tf_op jit(solution)/shard_map/all_gather | solution.py:46
  91.8 6.9 %reshape.50 = bf16[128,16384]{1,0:T(8,128)(2,1)} reshape(bf16[32,4,16384]{2,1,0:T(4,128)(2,1)} %all-gather.3.cloned.1.call-done) | data formatting | bytes 8388608
  98.7 4.8 %fusion = bf16[128,128]{0,1:T(8,128)(2,1)S(1)} fusion(bf16[16384,128]{1,0:T(8,128)(2,1)} %convert_element_type.26, bf16[128,16384]{1,0:T(8,128)(2,1)} %reshape.50), kind=kOutput, calls=%fused_computation.3 | convolution fusion | flops 536887296 | bytes 8421376 | tf_op jit(solution)/shard_map/dot_general | solution.py:18
  103.5 97.9 %psum.7 = bf16[128,128]{0,1:T(8,128)(2,1)S(1)} all-reduce(bf16[128,128]{0,1:T(8,128)(2,1)S(1)} %fusion), channel_id=1, replica_groups=mesh['voxel'=32,'feature'=4,'tm'=4] {'feature','tm'}, use_global_device_ids=true, to_apply=%region_0.1 | all-reduce | flops 16384 | bytes 65536 | tf_op jit(solution)/shard_map/psum | solution.py:48
  201.5 1.4 divide_convert_fusion
  (8 shorter events, 0.5 us)
Async XLA Ops:
  6.5 48.8 %copy-start = (bf16[768,2048]{1,0:T(8,128)(2,1)S(1)}, bf16[768,2048]{1,0:T(8,128)(2,1)}, u32[]{:S(2)}) copy-start(bf16[768,2048]{1,0:T(8,128)(2,1)} %param.7) | copy-start | bytes 9437188
  6.5 85.3 %all-gather.3.cloned.1.call-start = ((), (), s32[]{:S(2)}) async-start(), calls=%async_computation | async-start | bytes 4325376 | tf_op jit(solution)/shard_map/all_gather | solution.py:46
  21.8 31.9 %collective-permute-start = (bf16[12,128]{0,1:T(8,128)(2,1)S(1)}, bf16[12,128]{0,1:T(8,128)(2,1)S(1)}, u32[]{:S(2)}, u32[]{:S(2)}) collective-permute-start(bf16[12,128]{0,1:T(8,128)(2,1)S(1)} %copy.13), channel_id=1, source_target_pairs={{1,0},{2,1},{3,2},{5,4},{6,5},{7,6},{9,8},{10,9},{11,10},{13,12},{... | collective-permute-start | bytes 9224 | tf_op jit(solution)/shard_map/ppermute | solution.py:14
Sparse Core Ops, SparseCore 0:
  21.1 70.7 all-gather.2
where the time goes:
time: 211 us; the launch traced here: 210 us
  blocking collectives  112 us (53%)
  between operations  33.1 us (16%)
  local copies, waits for them, and re-layouts  24.3 us (12%)
  waiting for transfers between devices  17.7 us (8%)
  other arithmetic  11.2 us (5%)
  matrix products  9.75 us (5%)
    psum x1, blocking collectives, shards(): lax.psum(rotated_part.astype(jnp.bfloat16), ('feature', 'tm'))  97.9 us
    all_gather x1, waiting for transfers between devices, shards(): lax.all_gather(panel_rows, 'voxel', axis=1, tiled=True)  17.7 us
    all_gather x1, blocking collectives, shards(): panel_rows = lax.all_gather(panel, 'tm', axis=0, tiled=True)  14.4 us
    convert_element_type x2, local copies, waits for them, and re-layouts, shards(): partial_cov = cross.reshape(d_local * DELAYS, v_cols).astype(jnp.bfloat16)  13.8 us
    dot_general x2, matrix products, contract_rows(): lax.dot_general(left, right, (((0,), (0,)), ((), ())), preferred_element_...  9.75 us
    unnamed x4, local copies, waits for them, and re-layouts  7.98 us
    and x2, other arithmetic, shards(): valid = (positions + offset < total_rows) & (target_runs == own_runs)  6.84 us
  transfers between devices with their start and end apart: 2, of which 1 were waited for; matrix products, arithmetic and copies ran while one was open for 15% of the time, Pallas kernels for 0%

commit v1 on v0

--- a/solution.py
+++ b/solution.py
@@ -45,7 +45,9 @@
     rotated_part = contract_rows(
         lax.all_gather(panel_rows, "voxel", axis=1, tiled=True), partial_cov
     )
-    rotated = lax.psum(rotated_part.astype(jnp.bfloat16), ("feature", "tm")).astype(jnp.float32)
+    rotated = jnp.sum(
+        lax.all_gather(rotated_part.astype(jnp.bfloat16), ("feature", "tm")), axis=0
+    ).astype(jnp.float32)
     penalty = 2.0 ** ((ridge_grid.astype(jnp.float32) - 8.0) * 0.5)
     scaled = rotated[None] / (
         math.sqrt(total_rows) * (eigvals[None, :, None] + penalty[:, None, None])

time: 211 us -> 175 us (0.83)
  the two profiles are of different devices: /device:TPU:2 before, /device:TPU:4 now
where the time goes in v1:
time: 175 us; the launch traced here: 174 us
  blocking collectives  77.1 us (44%)
  between operations  33.2 us (19%)
  local copies, waits for them, and re-layouts  24.4 us (14%)
  waiting for transfers between devices  17.1 us (10%)
  other arithmetic  11.5 us (7%)
  matrix products  9.75 us (6%)
    all_gather x1, blocking collectives, shards(): lax.all_gather(rotated_part.astype(jnp.bfloat16), ('feature', 'tm'))  62.7 us
    all_gather x1, waiting for transfers between devices, shards(): lax.all_gather(panel_rows, 'voxel', axis=1, tiled=True)  17.1 us
    all_gather x1, blocking collectives, shards(): panel_rows = lax.all_gather(panel, 'tm', axis=0, tiled=True)  14.4 us
    convert_element_type x2, local copies, waits for them, and re-layouts, shards(): partial_cov = cross.reshape(d_local * DELAYS, v_cols).astype(jnp.bfloat16)  13.8 us
    dot_general x2, matrix products, contract_rows(): lax.dot_general(left, right, (((0,), (0,)), ((), ())), preferred_element_...  9.75 us
    unnamed x5, local copies, waits for them, and re-layouts  8.09 us
    and x2, other arithmetic, shards(): valid = (positions + offset < total_rows) & (target_runs == own_runs)  6.84 us
  transfers between devices with their start and end apart: 2, of which 1 were waited for; matrix products, arithmetic and copies ran while one was open for 18% of the time, Pallas kernels for 0%

profile of v1, /device:TPU:4, one launch (start us, length us, event | category | flops | bytes accessed | tf_op | source)
XLA Modules:
  0.0 174.4 jit_solution(2911597386046883841)
XLA Ops:
  6.5 14.4 %all_gather.12 = bf16[16384,4]{0,1:T(4,128)(2,1)} all-gather(bf16[4096,4]{0,1:T(4,128)(2,1)} %param.9), channel_id=1, replica_groups=mesh['voxel'=32,'feature'=4,'tm'=4] {'tm'}, dimensions={0}, use_global_device_ids=true | all-gather | bytes 163840 | tf_op jit(solution)/shard_map/all_gather | solution.py:44
  20.9 0.7 slice.28
  21.8 1.3 collective-permute-start
  23.1 1.6 fusion.49
  29.6 4.1 %fusion.48 = (pred[768]{0:T(1024)(128)(4,1)S(1)}, pred[768]{0:T(1024)(128)(4,1)S(1)}, pred[768]{0:T(1024)(128)(4,1)S(1)}, pred[768]{0:T(1024)(128)(4,1)S(1)}, pred[768]{0:T(1024)(128)(4,1)S(1)}) fusion(s32[]{:T(128)S(6)} %select_n.98, s32[3072]{0:T(1024)} %param.13, s32[]{:T(128)} %bitcast.14, s32[]{:T(128)S(6)} %mul.17, s32[]{:T(128)S(6)} %select_n.77, ...), kind=kLoop, calls=%fused_computation.78 | loop fusion | flops 16128 | bytes 22812 | tf_op jit(solution)/shard_map/and | solution.py:38
  33.7 0.7 multiply_power_fusion
  34.4 0.7 add_multiply_fusion
  35.1 2.7 %fusion.47 = (pred[768]{0:T(1024)(128)(4,1)S(1)}, pred[768]{0:T(1024)(128)(4,1)S(1)}, pred[768]{0:T(1024)(128)(4,1)S(1)}) fusion(s32[]{:T(128)S(6)} %select_n.95, s32[3072]{0:T(1024)} %param.13, s32[]{:T(128)} %bitcast.12, s32[]{:T(128)S(6)} %mul.17, s32[]{:T(128)S(6)} %select_n.77, s32[]{:T(128)S(6)} %select_n.80, s32[]{:T(128)} %bitcast.2, ...), kind=kLoop, calls=%fused_computation.77 | loop fusion | flops 9984 | bytes 20244 | tf_op jit(solution)/shard_map/and | solution.py:38
  38.5 1.1 copy.12
  53.9 0.2 fusion.12
  54.1 0.2 fusion.16
  54.3 0.2 fusion.20
  54.5 0.2 fusion.24
  54.7 0.2 fusion.28
  54.9 0.2 fusion.32
  55.3 5.0 %convert_bitcast_fusion = bf16[2048,1024]{0,1:T(8,128)(2,1)} fusion(bf16[768,1024]{0,1:T(8,128)(2,1)S(1)} %bitcast.59, bf16[768,2048]{1,0:T(8,128)(2,1)S(1)} %copy-done), kind=kOutput, calls=%fused_computation | convolution fusion | flops 3223322624 | bytes 8912896 | tf_op jit(solution)/shard_map/dot_general | solution.py:18
  60.3 6.4 %copy.13 = bf16[2048,1024]{1,0:T(8,128)(2,1)} copy(bf16[2048,1024]{0,1:T(8,128)(2,1)} %convert_bitcast_fusion) | data formatting | bytes 8388608 | tf_op jit(solution)/shard_map/convert_element_type | solution.py:43
  66.7 7.4 %convert_element_type.32 = bf16[16384,128]{1,0:T(8,128)(2,1)} reshape(bf16[2048,1024]{1,0:T(8,128)(2,1)} %copy.13) | data formatting | bytes 8388608 | tf_op jit(solution)/shard_map/convert_element_type | solution.py:43
  74.1 17.1 %all-gather.4.cloned.1.call-done = bf16[32,4,16384]{2,1,0:T(4,128)(2,1)} async-done(((bf16[1,4,16384]{2,1,0:T(4,128)(2,1)}), bf16[32,4,16384]{2,1,0:T(4,128)(2,1)}) %all-gather.4.cloned.1.call-update) | async-done | bytes 4194320 | tf_op jit(solution)/shard_map/all_gather | solution.py:46
  91.2 6.9 %reshape.53 = bf16[128,16384]{1,0:T(8,128)(2,1)} reshape(bf16[32,4,16384]{2,1,0:T(4,128)(2,1)} %all-gather.4.cloned.1.call-done) | data formatting | bytes 8388608
  98.1 4.8 %fusion = bf16[128,128]{0,1:T(8,128)(2,1)S(1)} fusion(bf16[16384,128]{1,0:T(8,128)(2,1)} %convert_element_type.32, bf16[128,16384]{1,0:T(8,128)(2,1)} %reshape.53), kind=kOutput, calls=%fused_computation.3 | convolution fusion | flops 536887296 | bytes 8421376 | tf_op jit(solution)/shard_map/dot_general | solution.py:18
  102.9 62.7 %all-gather = bf16[2048,128]{0,1:T(8,128)(2,1)S(1)} all-gather(bf16[128,128]{0,1:T(8,128)(2,1)S(1)} %fusion), channel_id=2, replica_groups=mesh['voxel'=32,'feature'=4,'tm'=4] {'feature','tm'}, dimensions={0}, use_global_device_ids=true | all-gather | bytes 557056 | tf_op jit(solution)/shard_map/all_gather | solution.py:49
  165.8 0.3 bitcast_reduce_fusion
  166.1 1.4 divide_convert_fusion
  (10 shorter events, 0.8 us)
Async XLA Ops:
  6.5 48.8 %copy-start = (bf16[768,2048]{1,0:T(8,128)(2,1)S(1)}, bf16[768,2048]{1,0:T(8,128)(2,1)}, u32[]{:S(2)}) copy-start(bf16[768,2048]{1,0:T(8,128)(2,1)} %param.7) | copy-start | bytes 9437188
  6.5 84.7 %all-gather.4.cloned.1.call-start = ((), (), s32[]{:S(2)}) async-start(), calls=%async_computation | async-start | bytes 4325376 | tf_op jit(solution)/shard_map/all_gather | solution.py:46
  21.8 31.9 %collective-permute-start = (bf16[12,128]{0,1:T(8,128)(2,1)S(1)}, bf16[12,128]{0,1:T(8,128)(2,1)S(1)}, u32[]{:S(2)}, u32[]{:S(2)}) collective-permute-start(bf16[12,128]{0,1:T(8,128)(2,1)S(1)} %copy.11), channel_id=1, source_target_pairs={{1,0},{2,1},{3,2},{5,4},{6,5},{7,6},{9,8},{10,9},{11,10},{13,12},{... | collective-permute-start | bytes 9224 | tf_op jit(solution)/shard_map/ppermute | solution.py:14
Sparse Core Ops, SparseCore 0:
  21.1 70.1 all-gather.3

commit v2 on v0

--- a/solution.py
+++ b/solution.py
@@ -45,7 +45,9 @@
     rotated_part = contract_rows(
         lax.all_gather(panel_rows, "voxel", axis=1, tiled=True), partial_cov
     )
-    rotated = lax.psum(rotated_part.astype(jnp.bfloat16), ("feature", "tm")).astype(jnp.float32)
+    rotated = lax.psum(lax.psum(rotated_part.astype(jnp.bfloat16), "tm"), "feature").astype(
+        jnp.float32
+    )
     penalty = 2.0 ** ((ridge_grid.astype(jnp.float32) - 8.0) * 0.5)
     scaled = rotated[None] / (
         math.sqrt(total_rows) * (eigvals[None, :, None] + penalty[:, None, None])

time: 211 us -> 156 us (0.74)
  blocking collectives: 112 us -> 57.1 us
    psum x1 -> x2, blocking collectives: 97.9 us -> 42.7 us  [the longest x1 25.5 us: shards(): lax.psum(lax.psum(rotated_part.astype(jnp.bfloat16), 'tm'), 'feature')]
  transfers between devices with their start and end apart: 2 -> 2, of which waited for: 1 -> 1; matrix products, arithmetic and copies ran while one was open for 15% -> 21% of each run, Pallas kernels for 0% -> 0%
where the time goes in v2:
time: 156 us; the launch traced here: 155 us
  blocking collectives  57.1 us (37%)
  between operations  33.1 us (21%)
  local copies, waits for them, and re-layouts  24.3 us (16%)
  waiting for transfers between devices  17.7 us (11%)
  other arithmetic  11.2 us (7%)
  matrix products  9.74 us (6%)
    psum x1, blocking collectives, shards(): lax.psum(lax.psum(rotated_part.astype(jnp.bfloat16), 'tm'), 'feature')  25.5 us
    all_gather x1, waiting for transfers between devices, shards(): lax.all_gather(panel_rows, 'voxel', axis=1, tiled=True)  17.7 us
    psum x1, blocking collectives, shards(): lax.psum(rotated_part.astype(jnp.bfloat16), 'tm')  17.2 us
    all_gather x1, blocking collectives, shards(): panel_rows = lax.all_gather(panel, 'tm', axis=0, tiled=True)  14.4 us
    convert_element_type x2, local copies, waits for them, and re-layouts, shards(): partial_cov = cross.reshape(d_local * DELAYS, v_cols).astype(jnp.bfloat16)  13.8 us
    dot_general x2, matrix products, contract_rows(): lax.dot_general(left, right, (((0,), (0,)), ((), ())), preferred_element_...  9.74 us
    unnamed x4, local copies, waits for them, and re-layouts  7.98 us
    and x2, other arithmetic, shards(): valid = (positions + offset < total_rows) & (target_runs == own_runs)  6.84 us
  transfers between devices with their start and end apart: 2, of which 1 were waited for; matrix products, arithmetic and copies ran while one was open for 21% of the time, Pallas kernels for 0%

profile of v2, /device:TPU:2, one launch (start us, length us, event | category | flops | bytes accessed | tf_op | source)
XLA Modules:
  0.0 154.5 jit_solution(17569672868686033391)
XLA Ops:
  6.5 14.4 %all_gather.6 = bf16[16384,4]{0,1:T(4,128)(2,1)} all-gather(bf16[4096,4]{0,1:T(4,128)(2,1)} %param.9), channel_id=1, replica_groups=mesh['voxel'=32,'feature'=4,'tm'=4] {'tm'}, dimensions={0}, use_global_device_ids=true | all-gather | bytes 163840 | tf_op jit(solution)/shard_map/all_gather | solution.py:44
  21.0 0.7 slice.28
  21.8 1.3 collective-permute-start
  23.1 1.6 %fusion.49 = (s32[1]{0:T(128)}, s32[1]{0:T(128)}, s32[1]{0:T(128)}, s32[1]{0:T(128)}, s32[1]{0:T(128)}, /*index=5*/s32[1]{0:T(128)}, s32[1]{0:T(128)}, s32[1]{0:T(128)}) fusion(s32[8]{0:T(128)} %param.12), kind=kLoop, calls=%fused_computation.79 | loop fusion | bytes 64 | tf_op jit(solution)/shard_map/slice | solution.py:36
  29.6 4.1 %fusion.48 = (pred[768]{0:T(1024)(128)(4,1)S(1)}, pred[768]{0:T(1024)(128)(4,1)S(1)}, pred[768]{0:T(1024)(128)(4,1)S(1)}, pred[768]{0:T(1024)(128)(4,1)S(1)}, pred[768]{0:T(1024)(128)(4,1)S(1)}) fusion(s32[]{:T(128)S(6)} %select_n.98, s32[3072]{0:T(1024)} %param.13, s32[]{:T(128)} %bitcast.14, s32[]{:T(128)S(6)} %mul.17, s32[]{:T(128)S(6)} %select_n.77, ...), kind=kLoop, calls=%fused_computation.77 | loop fusion | flops 16128 | bytes 22812 | tf_op jit(solution)/shard_map/and | solution.py:38
  33.7 0.7 multiply_power_fusion
  34.4 0.7 add_multiply_fusion
  35.1 2.8 %fusion.47 = (pred[768]{0:T(1024)(128)(4,1)S(1)}, pred[768]{0:T(1024)(128)(4,1)S(1)}, pred[768]{0:T(1024)(128)(4,1)S(1)}) fusion(s32[]{:T(128)S(6)} %select_n.95, s32[3072]{0:T(1024)} %param.13, s32[]{:T(128)} %bitcast.12, s32[]{:T(128)S(6)} %mul.17, s32[]{:T(128)S(6)} %select_n.77, s32[]{:T(128)S(6)} %select_n.80, s32[]{:T(128)} %bitcast.2, ...), kind=kLoop, calls=%fused_computation.76 | loop fusion | flops 9984 | bytes 20244 | tf_op jit(solution)/shard_map/and | solution.py:38
  38.5 1.1 copy.14
  53.9 0.2 fusion.12
  54.1 0.2 fusion.16
  54.3 0.2 fusion.20
  54.5 0.2 fusion.24
  54.7 0.2 fusion.28
  54.9 0.2 fusion.32
  55.3 5.0 %convert_bitcast_fusion = bf16[2048,1024]{0,1:T(8,128)(2,1)} fusion(bf16[768,1024]{0,1:T(8,128)(2,1)S(1)} %bitcast.53, bf16[768,2048]{1,0:T(8,128)(2,1)S(1)} %copy-done), kind=kOutput, calls=%fused_computation | convolution fusion | flops 3223322624 | bytes 8912896 | tf_op jit(solution)/shard_map/dot_general | solution.py:18
  60.3 6.4 %copy.15 = bf16[2048,1024]{1,0:T(8,128)(2,1)} copy(bf16[2048,1024]{0,1:T(8,128)(2,1)} %convert_bitcast_fusion) | data formatting | bytes 8388608 | tf_op jit(solution)/shard_map/convert_element_type | solution.py:43
  66.7 7.4 %convert_element_type.26 = bf16[16384,128]{1,0:T(8,128)(2,1)} reshape(bf16[2048,1024]{1,0:T(8,128)(2,1)} %copy.15) | data formatting | bytes 8388608 | tf_op jit(solution)/shard_map/convert_element_type | solution.py:43
  74.1 17.7 %all-gather.3.cloned.1.call-done = bf16[32,4,16384]{2,1,0:T(4,128)(2,1)} async-done(((bf16[1,4,16384]{2,1,0:T(4,128)(2,1)}), bf16[32,4,16384]{2,1,0:T(4,128)(2,1)}) %all-gather.3.cloned.1.call-update) | async-done | bytes 4194320 | tf_op jit(solution)/shard_map/all_gather | solution.py:46
  91.8 6.9 %reshape.50 = bf16[128,16384]{1,0:T(8,128)(2,1)} reshape(bf16[32,4,16384]{2,1,0:T(4,128)(2,1)} %all-gather.3.cloned.1.call-done) | data formatting | bytes 8388608
  98.7 4.8 %fusion = bf16[128,128]{0,1:T(8,128)(2,1)S(1)} fusion(bf16[16384,128]{1,0:T(8,128)(2,1)} %convert_element_type.26, bf16[128,16384]{1,0:T(8,128)(2,1)} %reshape.50), kind=kOutput, calls=%fused_computation.3 | convolution fusion | flops 536887296 | bytes 8421376 | tf_op jit(solution)/shard_map/dot_general | solution.py:18
  103.5 17.2 %psum.14 = bf16[128,128]{0,1:T(8,128)(2,1)S(1)} all-reduce(bf16[128,128]{0,1:T(8,128)(2,1)S(1)} %fusion), channel_id=1, replica_groups=mesh['voxel'=32,'feature'=4,'tm'=4] {'tm'}, use_global_device_ids=true, to_apply=%region_0.1 | all-reduce | flops 16384 | bytes 65536 | tf_op jit(solution)/shard_map/psum | solution.py:48
  120.7 25.5 %psum.15 = bf16[128,128]{0,1:T(8,128)(2,1)S(1)} all-reduce(bf16[128,128]{0,1:T(8,128)(2,1)S(1)} %psum.14), channel_id=1, replica_groups=mesh['voxel'=32,'feature'=4,'tm'=4] {'feature'}, use_global_device_ids=true, to_apply=%region_1.2 | all-reduce | flops 16384 | bytes 65536 | tf_op jit(solution)/shard_map/psum | solution.py:48
  146.3 1.4 divide_convert_fusion
  (9 shorter events, 0.7 us)
Async XLA Ops:
  6.5 48.8 %copy-start = (bf16[768,2048]{1,0:T(8,128)(2,1)S(1)}, bf16[768,2048]{1,0:T(8,128)(2,1)}, u32[]{:S(2)}) copy-start(bf16[768,2048]{1,0:T(8,128)(2,1)} %param.7) | copy-start | bytes 9437188
  6.5 85.3 %all-gather.3.cloned.1.call-start = ((), (), s32[]{:S(2)}) async-start(), calls=%async_computation | async-start | bytes 4325376 | tf_op jit(solution)/shard_map/all_gather | solution.py:46
  21.8 31.9 %collective-permute-start = (bf16[12,128]{0,1:T(8,128)(2,1)S(1)}, bf16[12,128]{0,1:T(8,128)(2,1)S(1)}, u32[]{:S(2)}, u32[]{:S(2)}) collective-permute-start(bf16[12,128]{0,1:T(8,128)(2,1)S(1)} %copy.13), channel_id=1, source_target_pairs={{1,0},{2,1},{3,2},{5,4},{6,5},{7,6},{9,8},{10,9},{11,10},{13,12},{... | collective-permute-start | bytes 9224 | tf_op jit(solution)/shard_map/ppermute | solution.py:14
Sparse Core Ops, SparseCore 0:
  21.1 70.6 all-gather.2
